TPU v7x, 32 devices: a whole 2x2x4 slice. The times are simulated.
32 devices in a mesh: grp: 4 (over z), mem: 8 (over y, x, core).
Axes of the slice: x: 2, y: 2, z: 4, core: 2. Of those that a mesh axis runs over, the one named last changes fastest.
Arguments:
- basis: float32 [20, 2048, 128], P(None, ('grp', 'mem'))
- precond: bfloat16 [2048, 128, 128], P(('grp', 'mem'))
- leaf_rows: float32 [1024, 128], P(('grp', 'mem')), may hold values from -6 to 6
- leaf_fiber: int32 [1024], P(('grp', 'mem')), may hold values from 0 to 63
- strad_rows: float32 [1024, 128], P(('grp', 'mem')), may hold values from -6 to 6
- strad_fiber: int32 [1024], P(('grp', 'mem')), may hold values from 0 to 63
- strad_count: int32 [32, 4], P(('grp', 'mem')), may hold values from 0 to 8, as said below
Outputs:
- coeffs: float32 [21], replicated
- next_vector: float32 [2048, 128], P(('grp', 'mem'))
Inputs may be any that keep to these rules, and one draw needn't show every extreme that they name: `leaf_fiber`: a destination fiber within the destination device. `strad_fiber`: a fiber of the receiving device. The first strad_count slots of a block are live, the rest are not read; some device fills a block.
All inputs are finite; a program needn't handle non-finite values.
Results may differ from a plain program's by a relative error of at most 0.0011.
Values sent between devices are 32-bit elements; how exact they have to be, the bound alone decides.
A program may use at most 64 MiB of HBM per device.

v0:
```python
import jax
import jax.numpy as jnp
from jax import lax
from jax.sharding import PartitionSpec as P

EPS = 1e-06


def local(basis, precond, leaf_rows, leaf_fiber, strad_rows, strad_fiber, strad_count):
    groups = lax.axis_size("grp")
    members = lax.axis_size("mem")
    krylov, fibers_here, width = basis.shape
    fiber_index = jnp.arange(fibers_here, dtype=jnp.int32)
    arrived, arrived_ids = (
        lax.all_to_all(leaf_rows, "mem", split_axis=0, concat_axis=0, tiled=True),
        lax.all_to_all(
            leaf_fiber.astype(jnp.float32), "mem", split_axis=0, concat_axis=0, tiled=True
        ),
    )
    select = (fiber_index[:, None] == arrived_ids.astype(jnp.int32)[None, :]).astype(jnp.float32)
    far_field = jnp.dot(
        select, arrived, precision=lax.Precision.HIGHEST, preferred_element_type=jnp.float32
    )
    strad_slots = strad_rows.shape[0] // groups
    keeping = (jnp.arange(strad_slots, dtype=jnp.int32)[None, :] < strad_count[0][:, None]).reshape(
        -1
    )
    outgoing = strad_rows * keeping[:, None].astype(jnp.float32)
    incoming = lax.all_to_all(outgoing, "grp", split_axis=0, concat_axis=0, tiled=True)
    select_near = (fiber_index[:, None] == strad_fiber[None, :]).astype(jnp.float32)
    near_field = jnp.dot(
        select_near, incoming, precision=lax.Precision.HIGHEST, preferred_element_type=jnp.float32
    )
    field = (basis[krylov - 1] + far_field + near_field).astype(jnp.bfloat16)
    applied = jnp.einsum("fij,fj->fi", precond, field, preferred_element_type=jnp.float32)
    total = float(fibers_here * width * groups * members)
    local_coef = jnp.einsum("kfi,fi->k", basis, applied, precision=lax.Precision.HIGHEST)
    gram_local = jnp.einsum("kfi,lfi->kl", basis, basis, precision=lax.Precision.HIGHEST)
    coef_sum, square_sum, gram_sum = lax.psum(
        (local_coef, jnp.sum(applied * applied), gram_local), ("grp", "mem")
    )
    coef = coef_sum / total
    gram = gram_sum / total
    residual = applied - jnp.einsum("k,kfi->fi", coef, basis, precision=lax.Precision.HIGHEST)
    projected = jnp.dot(gram, coef, precision=lax.Precision.HIGHEST)
    square = square_sum / total - 2.0 * jnp.sum(coef * coef) + jnp.sum(coef * projected)
    beta = jnp.sqrt(square + EPS)
    return (jnp.concatenate([coef, beta[None]]), residual / beta)


def solution(mesh):
    return jax.shard_map(
        local,
        mesh=mesh,
        in_specs=(
            P(None, ("grp", "mem"), None),
            P(("grp", "mem"), None, None),
            P(("grp", "mem"), None),
            P(("grp", "mem")),
            P(("grp", "mem"), None),
            P(("grp", "mem")),
            P(("grp", "mem"), None),
        ),
        out_specs=(P(), P(("grp", "mem"), None)),
        check_vma=False,
    )
```

profile of v0, /device:TPU:0, one launch (start us, length us, event | category | flops | bytes accessed | tf_op | source)
XLA Modules:
  0.0 79.5 jit_solution(3475346898591158441)
XLA Ops:
  0.6 0.0 copy-start
  0.7 0.8 %convert_element_type.29 = f32[32]{0:T(128)S(1)} convert(s32[32]{0:T(128)} %param.10) | non-fusion elementwise | flops 32 | bytes 256 | tf_op jit(solution)/shard_map/convert_element_type | solution.py:17
  1.5 0.7 all_to_all.22
  2.1 5.2 %all-to-all-start = ((f32[8,4,1]{1,2,0:T(1,128)}), f32[8,4,1]{1,2,0:T(1,128)S(1)}, u32[]{:S(2)}, u32[]{:S(2)}) async-start(f32[8,4,1]{1,2,0:T(1,128)} %bitcast.1), calls=%async_computation | async-start | bytes 8192 | tf_op jit(solution)/shard_map/all_to_all | solution.py:16
  7.3 0.7 fusion.16
  8.1 0.1 reshape.35
  8.2 1.4 %multiply_bitcast_fusion = f32[4,8,128]{2,1,0:T(8,128)} fusion(f32[32,128]{1,0:T(8,128)} %param.11, f32[32]{0:T(128)S(1)} %reshape.35), kind=kLoop, calls=%fused_computation.21 | loop fusion | flops 4096 | bytes 32896 | tf_op jit(solution)/shard_map/all_to_all | solution.py:29
  9.5 2.8 %convolution_bitcast_fusion = f32[20,20]{1,0:T(8,128)S(1)} fusion(f32[20,64,128]{2,1,0:T(8,128)} %param.7), kind=kOutput, calls=%fused_computation.4 | convolution fusion | flops 39321600 | bytes 656960 | tf_op jit(solution)/shard_map/kfi,lfi->kl/dot_general | solution.py:38
  12.3 4.2 %all-to-all-start.1 = ((f32[8,4,128]{2,1,0:T(4,128)}), f32[8,4,128]{2,1,0:T(4,128)S(1)}, u32[]{:S(2)}, u32[]{:S(2)}) async-start(f32[8,4,128]{2,1,0:T(4,128)} %bitcast.45), calls=%async_computation.1 | async-start | bytes 32768 | tf_op jit(solution)/shard_map/all_to_all | solution.py:15
  16.5 0.1 convert_element_type.31
  16.6 4.7 %all-to-all-done.1 = f32[8,4,128]{2,1,0:T(4,128)S(1)} async-done(((f32[8,4,128]{2,1,0:T(4,128)}), f32[8,4,128]{2,1,0:T(4,128)S(1)}, u32[]{:S(2)}, u32[]{:S(2)}) %all-to-all-start.1) | async-done | bytes 16416 | tf_op jit(solution)/shard_map/all_to_all | solution.py:15
  21.3 4.9 %all-to-all-start.2 = ((f32[4,8,128]{2,1,0:T(8,128)}), f32[4,8,128]{2,1,0:T(8,128)S(1)}, u32[]{:S(2)}, u32[]{:S(2)}) async-start(f32[4,8,128]{2,1,0:T(8,128)} %multiply_bitcast_fusion), calls=%async_computation.2 | async-start | bytes 32768 | tf_op jit(solution)/shard_map/all_to_all | solution.py:29
  26.2 0.9 %convolution_add_fusion.1 = f32[64,128]{1,0:T(8,128)S(1)} fusion(f32[32,128]{1,0:T(8,128)S(1)} %bitcast.44, f32[20,64,128]{2,1,0:T(8,128)} %param.7, s32[32]{0:T(128)S(1)} %convert_element_type.31), kind=kOutput, calls=%fused_computation.1 | convolution fusion | flops 3155968 | bytes 82048 | tf_op jit(solution)/shard_map/dot_general | solution.py:21
  27.1 4.7 %all-to-all-done.2 = f32[4,8,128]{2,1,0:T(8,128)S(1)} async-done(((f32[4,8,128]{2,1,0:T(8,128)}), f32[4,8,128]{2,1,0:T(8,128)S(1)}, u32[]{:S(2)}, u32[]{:S(2)}) %all-to-all-start.2) | async-done | bytes 16416 | tf_op jit(solution)/shard_map/all_to_all | solution.py:29
  31.8 0.8 %fusion.1 = bf16[64,128,1]{1,0,2:T(8,128)(2,1)S(1)} fusion(f32[64,128]{1,0:T(8,128)S(1)} %convolution_add_fusion.1, f32[4,8,128]{2,1,0:T(8,128)S(1)} %all-to-all-done.2, s32[32]{0:T(128)} %param.12), kind=kOutput, calls=%fused_computation.3 | convolution fusion | flops 3164160 | bytes 65664 | tf_op jit(solution)/shard_map/dot_general | solution.py:31
  32.6 1.2 %fusion.9 = f32[64,1,128]{2,1,0:T(1,128)S(1)} fusion(bf16[64,128,128]{2,1,0:T(8,128)(2,1)S(1)} %copy-done, bf16[64,128,1]{1,0,2:T(8,128)(2,1)S(1)} %fusion.1), kind=kOutput, calls=%fused_computation.14 | convolution fusion | flops 2097152 | bytes 2146304 | tf_op jit(solution)/shard_map/fij,fj->fi/dot_general | solution.py:35
  33.8 1.1 %convolution_bitcast_fusion.2 = f32[20]{0:T(128)S(1)} fusion(f32[20,64,128]{2,1,0:T(8,128)S(1)} %copy-done.1, f32[64,1,128]{2,1,0:T(1,128)S(1)} %fusion.9), kind=kOutput, calls=%fused_computation.7 | convolution fusion | flops 1966080 | bytes 688208 | tf_op jit(solution)/shard_map/kfi,fi->k/dot_general | solution.py:37
  34.8 0.6 multiply_reduce_fusion
  35.5 38.5 %all-reduce = (f32[]{:T(128)}, f32[20]{0:T(128)S(1)}, f32[20,20]{1,0:T(8,128)S(1)}) all-reduce(f32[]{:T(128)} %multiply_reduce_fusion, f32[20]{0:T(128)S(1)} %convolution_bitcast_fusion.2, f32[20,20]{1,0:T(8,128)S(1)} %convolution_bitcast_fusion), channel_id=1, replica_groups=mesh['grp'=4,'mem'=8] {'grp','mem'}, use_global_device_ids=true, to_apply=%region_2.0 | all-reduce | flops 421 | bytes 3368 | tf_op jit(solution)/shard_map/psum | solution.py:39
  74.0 0.6 broadcast_multiply_fusion
  74.6 0.9 %fusion.3 = f32[1,64,128]{2,0,1:T(1,128)S(1)} fusion(f32[20,64,128]{2,1,0:T(8,128)S(1)} %copy-done.1, f32[20]{0:T(128)S(1)} %get-tuple-element.3), kind=kOutput, calls=%fused_computation.8 | convolution fusion | flops 1966100 | bytes 688208 | tf_op jit(solution)/shard_map/k,kfi->fi/dot_general | solution.py:44
  75.5 0.8 %fusion.7 = f32[]{:T(128)} fusion(f32[20,20]{1,0:T(8,128)S(1)} %get-tuple-element.4, f32[20]{0:T(128)S(1)} %get-tuple-element.3), kind=kOutput, calls=%fused_computation.12 | convolution fusion | flops 5279 | bytes 1684 | tf_op jit(solution)/shard_map/dot_general | solution.py:45
  78.3 0.6 subtract_divide_fusion
  78.9 0.6 pad_maximum_fusion
  (5 shorter events, 0.0 us)
Async XLA Ops:
  0.6 31.9 %copy-start = (bf16[64,128,128]{2,1,0:T(8,128)(2,1)S(1)}, bf16[64,128,128]{2,1,0:T(8,128)(2,1)}, u32[]{:S(2)}) copy-start(bf16[64,128,128]{2,1,0:T(8,128)(2,1)} %param.8) | copy-start | bytes 6291460
  0.6 33.1 %copy-start.1 = (f32[20,64,128]{2,1,0:T(8,128)S(1)}, f32[20,64,128]{2,1,0:T(8,128)}, u32[]{:S(2)}) copy-start(f32[20,64,128]{2,1,0:T(8,128)} %param.7) | copy-start | bytes 1966084
  2.1 10.2 %all-to-all-start = ((f32[8,4,1]{1,2,0:T(1,128)}), f32[8,4,1]{1,2,0:T(1,128)S(1)}, u32[]{:S(2)}, u32[]{:S(2)}) async-start(f32[8,4,1]{1,2,0:T(1,128)} %bitcast.1), calls=%async_computation | async-start | bytes 8192 | tf_op jit(solution)/shard_map/all_to_all | solution.py:16
  12.3 9.0 %all-to-all-start.1 = ((f32[8,4,128]{2,1,0:T(4,128)}), f32[8,4,128]{2,1,0:T(4,128)S(1)}, u32[]{:S(2)}, u32[]{:S(2)}) async-start(f32[8,4,128]{2,1,0:T(4,128)} %bitcast.45), calls=%async_computation.1 | async-start | bytes 32768 | tf_op jit(solution)/shard_map/all_to_all | solution.py:15
  21.3 10.5 %all-to-all-start.2 = ((f32[4,8,128]{2,1,0:T(8,128)}), f32[4,8,128]{2,1,0:T(8,128)S(1)}, u32[]{:S(2)}, u32[]{:S(2)}) async-start(f32[4,8,128]{2,1,0:T(8,128)} %multiply_bitcast_fusion), calls=%async_computation.2 | async-start | bytes 32768 | tf_op jit(solution)/shard_map/all_to_all | solution.py:29
where the time goes:
time: 80.1 us; the launch traced here: 79.5 us
  blocking collectives  38.5 us (48%)
  starting transfers between devices  14.3 us (18%)
  waiting for transfers between devices  9.37 us (12%)
  matrix products  8.4 us (10%)
  other arithmetic  5.37 us (7%)
  between operations  2.73 us (3%)
  local copies, waits for them, and re-layouts  0.86 us (1%)
    psum x1, blocking collectives, local(): lax.psum((local_coef, jnp.sum(applied * applied), gram_local), ('grp', 'm...  38.5 us
    all_to_all x1, starting transfers between devices, local(): lax.all_to_all(leaf_fiber.astype(jnp.float32), 'mem', split_axis=0, conca...  5.2 us
    all_to_all x1, starting transfers between devices, local(): lax.all_to_all(outgoing, 'grp', split_axis=0, concat_axis=0, tiled=True)  4.88 us
    all_to_all x1, waiting for transfers between devices, local(): lax.all_to_all(outgoing, 'grp', split_axis=0, concat_axis=0, tiled=True)  4.71 us
    all_to_all x1, waiting for transfers between devices, local(): lax.all_to_all(leaf_rows, 'mem', split_axis=0, concat_axis=0, tiled=True)  4.65 us
    all_to_all x1, starting transfers between devices, local(): lax.all_to_all(leaf_rows, 'mem', split_axis=0, concat_axis=0, tiled=True)  4.21 us
    dot_general x1, matrix products, local(): jnp.einsum('kfi,lfi->kl', basis, basis, precision=lax.Precision.HIGHEST)  2.75 us
  transfers between devices with their start and end apart: 3, of which 2 were waited for; matrix products, arithmetic and copies ran while one was open for 7% of the time, Pallas kernels for 0%

commit v1 on v0

--- a/solution.py
+++ b/solution.py
@@ -37,7 +37,7 @@
     local_coef = jnp.einsum("kfi,fi->k", basis, applied, precision=lax.Precision.HIGHEST)
     gram_local = jnp.einsum("kfi,lfi->kl", basis, basis, precision=lax.Precision.HIGHEST)
     coef_sum, square_sum, gram_sum = lax.psum(
-        (local_coef, jnp.sum(applied * applied), gram_local), ("grp", "mem")
+        lax.psum((local_coef, jnp.sum(applied * applied), gram_local), "grp"), "mem"
     )
     coef = coef_sum / total
     gram = gram_sum / total

time: 80.1 us -> 82.1 us (1.025)
  blocking collectives: 38.5 us -> 40.5 us
    psum x1 -> x2, blocking collectives: 38.5 us -> 40.5 us  [the longest x1 23.4 us: local(): lax.psum(lax.psum((local_coef, jnp.sum(applied * applied), gram_local), '...]
where the time goes in v1:
time: 82.1 us; the launch traced here: 81.5 us
  blocking collectives  40.5 us (49%)
  starting transfers between devices  14.3 us (17%)
  waiting for transfers between devices  9.37 us (11%)
  matrix products  8.4 us (10%)
  other arithmetic  5.37 us (7%)
  between operations  2.73 us (3%)
  local copies, waits for them, and re-layouts  0.86 us (1%)
    psum x1, blocking collectives, local(): lax.psum(lax.psum((local_coef, jnp.sum(applied * applied), gram_local), '...  23.4 us
    psum x1, blocking collectives, local(): lax.psum((local_coef, jnp.sum(applied * applied), gram_local), 'grp')  17.1 us
    all_to_all x1, starting transfers between devices, local(): lax.all_to_all(leaf_fiber.astype(jnp.float32), 'mem', split_axis=0, conca...  5.2 us
    all_to_all x1, starting transfers between devices, local(): lax.all_to_all(outgoing, 'grp', split_axis=0, concat_axis=0, tiled=True)  4.88 us
    all_to_all x1, waiting for transfers between devices, local(): lax.all_to_all(outgoing, 'grp', split_axis=0, concat_axis=0, tiled=True)  4.71 us
    all_to_all x1, waiting for transfers between devices, local(): lax.all_to_all(leaf_rows, 'mem', split_axis=0, concat_axis=0, tiled=True)  4.65 us
    all_to_all x1, starting transfers between devices, local(): lax.all_to_all(leaf_rows, 'mem', split_axis=0, concat_axis=0, tiled=True)  4.21 us
    dot_general x1, matrix products, local(): jnp.einsum('kfi,lfi->kl', basis, basis, precision=lax.Precision.HIGHEST)  2.75 us
  transfers between devices with their start and end apart: 3, of which 2 were waited for; matrix products, arithmetic and copies ran while one was open for 7% of the time, Pallas kernels for 0%

profile of v1, /device:TPU:0, one launch (start us, length us, event | category | flops | bytes accessed | tf_op | source)
XLA Modules:
  0.0 81.5 jit_solution(2610280801536276341)
XLA Ops:
  0.7 0.8 convert_element_type.29
  1.5 0.7 all_to_all.22
  2.1 5.2 %all-to-all-start = ((f32[8,4,1]{1,2,0:T(1,128)}), f32[8,4,1]{1,2,0:T(1,128)S(1)}, u32[]{:S(2)}, u32[]{:S(2)}) async-start(f32[8,4,1]{1,2,0:T(1,128)} %bitcast.1), calls=%async_computation | async-start | bytes 8192 | tf_op jit(solution)/shard_map/all_to_all | solution.py:16
  7.3 0.7 fusion.16
  8.1 0.1 reshape.35
  8.2 1.4 %multiply_bitcast_fusion = f32[4,8,128]{2,1,0:T(8,128)} fusion(f32[32,128]{1,0:T(8,128)} %param.11, f32[32]{0:T(128)S(1)} %reshape.35), kind=kLoop, calls=%fused_computation.21 | loop fusion | flops 4096 | bytes 32896 | tf_op jit(solution)/shard_map/all_to_all | solution.py:29
  9.5 2.8 %convolution_bitcast_fusion = f32[20,20]{1,0:T(8,128)S(1)} fusion(f32[20,64,128]{2,1,0:T(8,128)} %param.7), kind=kOutput, calls=%fused_computation.4 | convolution fusion | flops 39321600 | bytes 656960 | tf_op jit(solution)/shard_map/kfi,lfi->kl/dot_general | solution.py:38
  12.3 4.2 %all-to-all-start.1 = ((f32[8,4,128]{2,1,0:T(4,128)}), f32[8,4,128]{2,1,0:T(4,128)S(1)}, u32[]{:S(2)}, u32[]{:S(2)}) async-start(f32[8,4,128]{2,1,0:T(4,128)} %bitcast.45), calls=%async_computation.1 | async-start | bytes 32768 | tf_op jit(solution)/shard_map/all_to_all | solution.py:15
  16.5 0.1 convert_element_type.31
  16.6 4.7 %all-to-all-done.1 = f32[8,4,128]{2,1,0:T(4,128)S(1)} async-done(((f32[8,4,128]{2,1,0:T(4,128)}), f32[8,4,128]{2,1,0:T(4,128)S(1)}, u32[]{:S(2)}, u32[]{:S(2)}) %all-to-all-start.1) | async-done | bytes 16416 | tf_op jit(solution)/shard_map/all_to_all | solution.py:15
  21.3 4.9 %all-to-all-start.2 = ((f32[4,8,128]{2,1,0:T(8,128)}), f32[4,8,128]{2,1,0:T(8,128)S(1)}, u32[]{:S(2)}, u32[]{:S(2)}) async-start(f32[4,8,128]{2,1,0:T(8,128)} %multiply_bitcast_fusion), calls=%async_computation.2 | async-start | bytes 32768 | tf_op jit(solution)/shard_map/all_to_all | solution.py:29
  26.2 0.9 %convolution_add_fusion.1 = f32[64,128]{1,0:T(8,128)S(1)} fusion(f32[32,128]{1,0:T(8,128)S(1)} %bitcast.44, f32[20,64,128]{2,1,0:T(8,128)} %param.7, s32[32]{0:T(128)S(1)} %convert_element_type.31), kind=kOutput, calls=%fused_computation.1 | convolution fusion | flops 3155968 | bytes 82048 | tf_op jit(solution)/shard_map/dot_general | solution.py:21
  27.1 4.7 %all-to-all-done.2 = f32[4,8,128]{2,1,0:T(8,128)S(1)} async-done(((f32[4,8,128]{2,1,0:T(8,128)}), f32[4,8,128]{2,1,0:T(8,128)S(1)}, u32[]{:S(2)}, u32[]{:S(2)}) %all-to-all-start.2) | async-done | bytes 16416 | tf_op jit(solution)/shard_map/all_to_all | solution.py:29
  31.8 0.8 fusion.1
  32.6 1.2 %fusion.9 = f32[64,1,128]{2,1,0:T(1,128)S(1)} fusion(bf16[64,128,128]{2,1,0:T(8,128)(2,1)S(1)} %copy-done, bf16[64,128,1]{1,0,2:T(8,128)(2,1)S(1)} %fusion.1), kind=kOutput, calls=%fused_computation.14 | convolution fusion | flops 2097152 | bytes 2146304 | tf_op jit(solution)/shard_map/fij,fj->fi/dot_general | solution.py:35
  33.8 1.1 %convolution_bitcast_fusion.2 = f32[20]{0:T(128)S(1)} fusion(f32[20,64,128]{2,1,0:T(8,128)S(1)} %copy-done.1, f32[64,1,128]{2,1,0:T(1,128)S(1)} %fusion.9), kind=kOutput, calls=%fused_computation.7 | convolution fusion | flops 1966080 | bytes 688208 | tf_op jit(solution)/shard_map/kfi,fi->k/dot_general | solution.py:37
  34.8 0.6 multiply_reduce_fusion
  35.5 17.1 %all-reduce.1 = (f32[]{:T(128)}, f32[20]{0:T(128)S(1)}, f32[20,20]{1,0:T(8,128)S(1)}) all-reduce(f32[]{:T(128)} %multiply_reduce_fusion, f32[20]{0:T(128)S(1)} %convolution_bitcast_fusion.2, f32[20,20]{1,0:T(8,128)S(1)} %convolution_bitcast_fusion), channel_id=1, replica_groups=mesh['grp'=4,'mem'=8] {'grp'}, use_global_device_ids=true, to_apply=%region_3.0 | all-reduce | flops 421 | bytes 3368 | tf_op jit(solution)/shard_map/psum | solution.py:40
  52.6 23.4 %all-reduce = (f32[]{:T(128)}, f32[20]{0:T(128)S(1)}, f32[20,20]{1,0:T(8,128)S(1)}) all-reduce(f32[]{:T(128)} %get-tuple-element.5, f32[20]{0:T(128)S(1)} %get-tuple-element.6, f32[20,20]{1,0:T(8,128)S(1)} %get-tuple-element.7), channel_id=1, replica_groups=mesh['grp'=4,'mem'=8] {'mem'}, use_global_device_ids=true, to_apply=%region_4.0 | all-reduce | flops 421 | bytes 3368 | tf_op jit(solution)/shard_map/psum | solution.py:39
  76.0 0.6 broadcast_multiply_fusion
  76.6 0.9 %fusion.3 = f32[1,64,128]{2,0,1:T(1,128)S(1)} fusion(f32[20,64,128]{2,1,0:T(8,128)S(1)} %copy-done.1, f32[20]{0:T(128)S(1)} %get-tuple-element.3), kind=kOutput, calls=%fused_computation.8 | convolution fusion | flops 1966100 | bytes 688208 | tf_op jit(solution)/shard_map/k,kfi->fi/dot_general | solution.py:44
  77.5 0.8 %fusion.7 = f32[]{:T(128)} fusion(f32[20,20]{1,0:T(8,128)S(1)} %get-tuple-element.4, f32[20]{0:T(128)S(1)} %get-tuple-element.3), kind=kOutput, calls=%fused_computation.12 | convolution fusion | flops 5279 | bytes 1684 | tf_op jit(solution)/shard_map/dot_general | solution.py:45
  80.3 0.6 subtract_divide_fusion
  80.9 0.6 pad_maximum_fusion
  (6 shorter events, 0.0 us)
Async XLA Ops:
  0.6 31.9 %copy-start = (bf16[64,128,128]{2,1,0:T(8,128)(2,1)S(1)}, bf16[64,128,128]{2,1,0:T(8,128)(2,1)}, u32[]{:S(2)}) copy-start(bf16[64,128,128]{2,1,0:T(8,128)(2,1)} %param.8) | copy-start | bytes 6291460
  0.6 33.1 %copy-start.1 = (f32[20,64,128]{2,1,0:T(8,128)S(1)}, f32[20,64,128]{2,1,0:T(8,128)}, u32[]{:S(2)}) copy-start(f32[20,64,128]{2,1,0:T(8,128)} %param.7) | copy-start | bytes 1966084
  2.1 10.2 %all-to-all-start = ((f32[8,4,1]{1,2,0:T(1,128)}), f32[8,4,1]{1,2,0:T(1,128)S(1)}, u32[]{:S(2)}, u32[]{:S(2)}) async-start(f32[8,4,1]{1,2,0:T(1,128)} %bitcast.1), calls=%async_computation | async-start | bytes 8192 | tf_op jit(solution)/shard_map/all_to_all | solution.py:16
  12.3 9.0 %all-to-all-start.1 = ((f32[8,4,128]{2,1,0:T(4,128)}), f32[8,4,128]{2,1,0:T(4,128)S(1)}, u32[]{:S(2)}, u32[]{:S(2)}) async-start(f32[8,4,128]{2,1,0:T(4,128)} %bitcast.45), calls=%async_computation.1 | async-start | bytes 32768 | tf_op jit(solution)/shard_map/all_to_all | solution.py:15
  21.3 10.5 %all-to-all-start.2 = ((f32[4,8,128]{2,1,0:T(8,128)}), f32[4,8,128]{2,1,0:T(8,128)S(1)}, u32[]{:S(2)}, u32[]{:S(2)}) async-start(f32[4,8,128]{2,1,0:T(8,128)} %multiply_bitcast_fusion), calls=%async_computation.2 | async-start | bytes 32768 | tf_op jit(solution)/shard_map/all_to_all | solution.py:29
